TPU v7x, 32 devices: a whole 2x2x4 slice. The times are simulated.
32 devices in a mesh: row: 2 (over x), col: 4 (over z), depth: 4 (over y, core).
Axes of the slice: x: 2, y: 2, z: 4, core: 2. Of those that a mesh axis runs over, the one named last changes fastest.
Arguments:
- inputs: bfloat16 [128, 5120], P(('row', 'depth'), 'col'), may hold values from -6 to 6
- targets: bfloat16 [128, 5120], P(('row', 'depth'), 'col'), may hold values from -6 to 6
- norm_gain: float32 [5120], P('col'), may hold values from 0.5 to 1.5
- w_gate: bfloat16 [5120, 8192], P('col', ('row', 'depth')), may hold values from -0.078125 to 0.078125
- w_up: bfloat16 [5120, 8192], P('col', ('row', 'depth')), may hold values from -0.078125 to 0.078125
- w_down: bfloat16 [8192, 5120], P(('row', 'depth'), 'col'), may hold values from -0.0625 to 0.0625
- probe_gate: bfloat16 [5120, 8192], P('col', ('row', 'depth')), may hold values from -1 to 1, as said below
- probe_up: bfloat16 [5120, 8192], P('col', ('row', 'depth')), may hold values from -1 to 1, as said below
- probe_down: bfloat16 [8192, 5120], P(('row', 'depth'), 'col'), may hold values from -1 to 1, as said below
- moment_gate: float32 [5120, 8192], P('col', ('row', 'depth')), may hold values from -18 to 18
- moment_up: float32 [5120, 8192], P('col', ('row', 'depth')), may hold values from -18 to 18
- moment_down: float32 [8192, 5120], P(('row', 'depth'), 'col'), may hold values from -18 to 18
- second_gate: float32 [5120, 8192], P('col', ('row', 'depth')), may hold values from 1 to 100
- second_up: float32 [5120, 8192], P('col', ('row', 'depth')), may hold values from 1 to 100
- second_down: float32 [8192, 5120], P(('row', 'depth'), 'col'), may hold values from 1 to 100
Outputs:
- new_moment_gate: float32 [5120, 8192], P('col', ('row', 'depth'))
- new_moment_up: float32 [5120, 8192], P('col', ('row', 'depth'))
- new_moment_down: float32 [8192, 5120], P(('row', 'depth'), 'col')
- new_second_gate: float32 [5120, 8192], P('col', ('row', 'depth'))
- new_second_up: float32 [5120, 8192], P('col', ('row', 'depth'))
- new_second_down: float32 [8192, 5120], P(('row', 'depth'), 'col')
- step_gate: float32 [5120, 8192], P('col', ('row', 'depth'))
- step_up: float32 [5120, 8192], P('col', ('row', 'depth'))
- step_down: float32 [8192, 5120], P(('row', 'depth'), 'col')
Inputs may be any that keep to these rules, and one draw needn't show every extreme that they name: `probe_gate`: every entry is +1 or -1. `probe_up`: every entry is +1 or -1. `probe_down`: every entry is +1 or -1.
All inputs are finite; a program needn't handle non-finite values.
Results may differ from a plain program's by a relative error of at most 0.0046.
Values may be sent and summed in bfloat16 or wider, within the bound.
A program may use at most 192 MiB of HBM per device.

v0:
```python
import jax
import jax.numpy as jnp
from jax import lax
from jax.sharding import PartitionSpec as P

D = 5120
TILE = 128
STEP = 1000


beta_one = 0.9
beta_two = 0.999
adam_floor = 1e-08
norm_floor = 1e-05


def silu_parts(gate_pre):
    sig = jax.nn.sigmoid(gate_pre)
    act = gate_pre * sig
    slope = sig * (1.0 + gate_pre * (1.0 - sig))
    bend = sig * (1.0 - sig) * (2.0 + gate_pre * (1.0 - 2.0 * sig))
    return (act, slope, bend)


def tile_means(product):
    height, breadth = product.shape
    blocks = product.reshape(height // TILE, TILE, breadth // TILE, TILE)
    means = jnp.mean(blocks, axis=(1, 3), keepdims=True)
    return jnp.broadcast_to(means, blocks.shape).reshape(height, breadth)


def adahessian(moment, second, gradient, curvature, probe):
    averaged = tile_means(probe.astype(jnp.float32) * curvature)
    new_moment = beta_one * moment + (1.0 - beta_one) * gradient
    new_second = beta_two * second + (1.0 - beta_two) * averaged * averaged
    corrected = new_moment / (1.0 - beta_one**STEP)
    scale_root = jnp.sqrt(new_second / (1.0 - beta_two**STEP))
    return (new_moment, new_second, corrected / (scale_root + adam_floor))


def matmul(left, right):
    return jnp.dot(left, right, preferred_element_type=jnp.float32)


def inner_left(left, right):
    return lax.dot_general(
        left, right, (((0,), (0,)), ((), ())), preferred_element_type=jnp.float32
    )


def inner_right(left, right):
    return lax.dot_general(
        left, right, (((1,), (1,)), ((), ())), preferred_element_type=jnp.float32
    )


def shards(
    inputs,
    targets,
    norm_gain,
    w_gate,
    w_up,
    w_down,
    probe_gate,
    probe_up,
    probe_down,
    moment_gate,
    moment_up,
    moment_down,
    second_gate,
    second_up,
    second_down,
):
    feats = inputs.astype(jnp.float32)
    local_width = feats.shape[1]
    squares = lax.psum(jnp.sum(feats * feats, axis=1), "col")
    scaling = lax.rsqrt(squares / D + norm_floor)
    normed_rows = (feats * scaling[:, None] * norm_gain).astype(jnp.bfloat16)
    normed = lax.all_gather(normed_rows, ("row", "depth"), axis=0, tiled=True)
    gate_pre, up_pre, gate_tan, up_tan = lax.psum(
        (
            matmul(normed, w_gate),
            matmul(normed, w_up),
            matmul(normed, probe_gate),
            matmul(normed, probe_up),
        ),
        "col",
    )
    act, slope, bend = silu_parts(gate_pre)
    hidden = (act * up_pre).astype(jnp.bfloat16)
    hidden_tan = (slope * gate_tan * up_pre + act * up_tan).astype(jnp.bfloat16)
    primal = matmul(hidden, w_down)
    tangent = matmul(hidden_tan, w_down) + matmul(hidden, probe_down)
    summed = lax.psum_scatter(
        jnp.concatenate([primal, tangent], axis=1),
        ("row", "depth"),
        scatter_dimension=0,
        tiled=True,
    )
    outputs = summed[:, :local_width] + feats
    error_rows = (outputs - targets.astype(jnp.float32)).astype(jnp.bfloat16)
    tangent_rows = summed[:, local_width:].astype(jnp.bfloat16)
    error, error_tan = (
        lax.all_gather(error_rows, ("row", "depth"), axis=0, tiled=True),
        lax.all_gather(tangent_rows, ("row", "depth"), axis=0, tiled=True),
    )
    back_hidden, back_tan = lax.psum(
        (
            inner_right(error, w_down),
            inner_right(error_tan, w_down) + inner_right(error, probe_down),
        ),
        "col",
    )
    back_gate = (back_hidden * up_pre * slope).astype(jnp.bfloat16)
    back_up = (back_hidden * act).astype(jnp.bfloat16)
    gate_tan_back = (
        back_tan * up_pre * slope
        + back_hidden * up_tan * slope
        + back_hidden * up_pre * bend * gate_tan
    ).astype(jnp.bfloat16)
    up_tan_back = (back_tan * act + back_hidden * slope * gate_tan).astype(jnp.bfloat16)
    grad_gate = inner_left(normed, back_gate)
    grad_up = inner_left(normed, back_up)
    grad_down = inner_left(hidden, error)
    curve_gate = inner_left(normed, gate_tan_back)
    curve_up = inner_left(normed, up_tan_back)
    curve_down = inner_left(hidden_tan, error) + inner_left(hidden, error_tan)
    gate_moment, gate_second, gate_step = adahessian(
        moment_gate, second_gate, grad_gate, curve_gate, probe_gate
    )
    up_moment, up_second, up_step = adahessian(moment_up, second_up, grad_up, curve_up, probe_up)
    down_moment, down_second, down_step = adahessian(
        moment_down, second_down, grad_down, curve_down, probe_down
    )
    return (
        gate_moment,
        up_moment,
        down_moment,
        gate_second,
        up_second,
        down_second,
        gate_step,
        up_step,
        down_step,
    )


def solution(mesh):
    return jax.shard_map(
        shards,
        mesh=mesh,
        in_specs=(
            P(("row", "depth"), "col"),
            P(("row", "depth"), "col"),
            P("col"),
            P("col", ("row", "depth")),
            P("col", ("row", "depth")),
            P(("row", "depth"), "col"),
            P("col", ("row", "depth")),
            P("col", ("row", "depth")),
            P(("row", "depth"), "col"),
            P("col", ("row", "depth")),
            P("col", ("row", "depth")),
            P(("row", "depth"), "col"),
            P("col", ("row", "depth")),
            P("col", ("row", "depth")),
            P(("row", "depth"), "col"),
        ),
        out_specs=(
            P("col", ("row", "depth")),
            P("col", ("row", "depth")),
            P(("row", "depth"), "col"),
            P("col", ("row", "depth")),
            P("col", ("row", "depth")),
            P(("row", "depth"), "col"),
            P("col", ("row", "depth")),
            P("col", ("row", "depth")),
            P(("row", "depth"), "col"),
        ),
        check_vma=False,
    )
```

profile of v0, /device:TPU:29, one launch (start us, length us, event | category | flops | bytes accessed | tf_op | source)
XLA Modules:
  0.0 310.2 jit_solution(7408397132917821951)
XLA Ops:
  8.3 6.4 %psum.49 = f32[16]{0:T(128)S(1)} all-reduce(f32[16]{0:T(128)S(1)} %fusion.16), channel_id=1, replica_groups=mesh['row'=2,'col'=4,'depth'=4] {'col'}, use_global_device_ids=true, to_apply=%region_1.0 | all-reduce | flops 16 | bytes 128 | tf_op jit(solution)/shard_map/psum | solution.py:76
  15.7 11.7 %all_gather.9 = bf16[128,1280]{1,0:T(8,128)(2,1)S(1)} all-gather(bf16[16,1280]{1,0:T(8,128)(2,1)S(1)} %fusion.18), channel_id=1, replica_groups=mesh['row'=2,'col'=4,'depth'=4] {'row','depth'}, dimensions={0}, use_global_device_ids=true | all-gather | bytes 368640 | tf_op jit(solution)/shard_map/all_gather | solution.py:79
  27.4 3.2 %fusion.35 = f32[128,1024]{1,0:T(8,128)} fusion(bf16[128,1280]{1,0:T(8,128)(2,1)S(1)} %all_gather.9, bf16[1280,1024]{1,0:T(8,128)(2,1)} %param.22), kind=kOutput, calls=%fused_computation.60 | convolution fusion | flops 335544320 | bytes 3473408 | tf_op jit(solution)/shard_map/dot_general | solution.py:42
  30.6 3.0 fusion.32
  36.3 84.8 %all-reduce.7.cloned.1.call-done = (f32[128,1024]{1,0:T(8,128)}, f32[128,1024]{1,0:T(8,128)}, f32[128,1024]{1,0:T(8,128)}, f32[128,1024]{1,0:T(8,128)}) async-done(((f32[128,1024]{1,0:T(8,128)}, f32[128,1024]{1,0:T(8,128)}, f32[128,1024]{1,0:T(8,128)}, f32[128,1024]{1,0:T(8,128)}), (f32[128,1024]{1,0:T(8,128)}, f32[128,1024]{1,0:T(8,128)}, f32[128,1024]{1,0:T(8,128)}, ...) | async-done | bytes 2097168 | tf_op jit(solution)/shard_map/psum | solution.py:80
  121.1 1.9 multiply_convert_fusion.2
  126.0 37.9 %reduce-scatter.2.cloned.1.call-done = f32[16,2560]{1,0:T(8,128)} async-done(((f32[128,2560]{1,0:T(8,128)}), f32[16,2560]{1,0:T(8,128)}) %reduce-scatter.2.cloned.1.call-update) | async-done | bytes 163856 | tf_op jit(solution)/shard_map/reduce_scatter | solution.py:94
  164.8 9.3 %all_gather.10 = bf16[128,1280]{1,0:T(8,128)(2,1)S(1)} all-gather(bf16[16,1280]{1,0:T(8,128)(2,1)S(1)} %fusion.20), channel_id=1, replica_groups=mesh['row'=2,'col'=4,'depth'=4] {'row','depth'}, dimensions={0}, use_global_device_ids=true | all-gather | bytes 368640 | tf_op jit(solution)/shard_map/all_gather | solution.py:104
  174.0 1.8 fusion.37
  175.8 4.3 %fusion.39 = f32[1024,1280]{1,0:T(8,128)} fusion(bf16[128,1024]{1,0:T(8,128)(2,1)} %copy-done.9, bf16[128,1280]{1,0:T(8,128)(2,1)S(1)} %all_gather.10), kind=kOutput, calls=%fused_computation.64 | convolution fusion | flops 335544320 | bytes 5832704 | tf_op jit(solution)/shard_map/dot_general | solution.py:46
  181.0 9.4 %all_gather.11 = bf16[128,1280]{1,0:T(8,128)(2,1)S(1)} all-gather(bf16[16,1280]{1,0:T(8,128)(2,1)S(1)} %slice.13), channel_id=1, replica_groups=mesh['row'=2,'col'=4,'depth'=4] {'row','depth'}, dimensions={0}, use_global_device_ids=true | all-gather | bytes 368640 | tf_op jit(solution)/shard_map/all_gather | solution.py:105
  192.1 1.8 convolution_add_fusion.1
  193.9 6.6 %add_multiply_fusion = f32[1024,1280]{1,0:T(8,128)} fusion(f32[1024,1280]{1,0:T(8,128)} %fusion.39, bf16[1024,1280]{1,0:T(8,128)(2,1)} %param.23, bf16[128,1024]{1,0:T(8,128)(2,1)S(1)} %get-tuple-element.21, bf16[128,1280]{1,0:T(8,128)(2,1)} %copy-done.10), kind=kOutput, calls=%fused_computation.12 | convolution fusion | flops 339476480 | bytes 13697024 | tf_op jit(solution)/shard_map/dot_general | solution.py:46
  200.5 5.9 %copy.24 = f32[1024,1280]{0,1:T(8,128)} copy(f32[1024,1280]{1,0:T(8,128)} %add_multiply_fusion) | data formatting | bytes 10485760 | tf_op jit(solution)/shard_map/mul | solution.py:33
  206.4 6.1 %copy.31 = f32[160,8,8,128]{3,2,1,0:T(8,128)} copy(f32[160,8,8,128]{3,1,2,0:T(8,128)} %bitcast.65) | data formatting | bytes 10485760
  212.5 2.9 reduce_sum.39
  215.8 3.6 %copy.38 = f32[160,8,8,128]{3,1,2,0:T(8,128)} copy(f32[160,8,8,128]{3,2,1,0:T(8,128)S(1)} %bitcast.66) | data formatting | bytes 10485760
  219.5 5.9 %copy.25 = f32[1024,1280]{1,0:T(8,128)} copy(f32[1024,1280]{0,1:T(8,128)} %bitcast.67) | data formatting | bytes 10485760 | tf_op jit(solution)/shard_map/reshape | solution.py:29
  225.4 10.8 %add_divide_fusion = (f32[1024,1280]{1,0:T(8,128)}, f32[1024,1280]{1,0:T(8,128)}, f32[1024,1280]{1,0:T(8,128)}) fusion(f32[1024,1280]{1,0:T(8,128)} %copy.25, f32[1024,1280]{1,0:T(8,128)} %param.29, bf16[128,1024]{1,0:T(8,128)(2,1)S(1)} %get-tuple-element.21, bf16[128,1280]{1,0:T(8,128)(2,1)S(1)} %all_gather.10, f32[1024,1280]{1,0:T(8,128)} %param.26), kind=kOutput, calls=%fused_computation.9 | convolution fusion | flops 348651520 | bytes 32047104 | tf_op jit(solution)/shard_map/dot_general | solution.py:46
  236.2 39.3 %all-reduce.5.cloned.1.call-done = (f32[128,1024]{1,0:T(8,128)}, f32[128,1024]{1,0:T(8,128)}) async-done(((f32[128,1024]{1,0:T(8,128)}, f32[128,1024]{1,0:T(8,128)}), (f32[128,1024]{1,0:T(8,128)}, f32[128,1024]{1,0:T(8,128)})) %all-reduce.5.cloned.1.call-update) | async-done | bytes 1048592 | tf_op jit(solution)/shard_map/psum | solution.py:107
  275.5 3.0 multiply_bitcast_fusion.1
  281.4 1.3 copy.29
  285.7 7.4 %add_divide_fusion.2 = (f32[1280,1024]{1,0:T(8,128)}, f32[1280,1024]{1,0:T(8,128)}, f32[1280,1024]{1,0:T(8,128)}) fusion(f32[160,8,8,128]{3,2,1,0:T(8,128)S(1)} %bitcast.71, f32[1280,1024]{1,0:T(8,128)S(1)} %bitcast.73, bf16[128,1280]{1,0:T(8,128)(2,1)S(1)} %all_gather.9, f32[128,1024]{1,0:T(8,128)S(1)} %copy-done.13, f32[128,1024]{1,0:T(8,128)S(1)} %copy-done.12, ...), kind=kOutput, calls=%fused_computation.11 | convolution fusion | flops 349962240 | bytes 33357824 | tf_op jit(solution)/shard_map/dot_general | solution.py:46
  293.5 10.1 %add_divide_fusion.1 = (f32[1280,1024]{1,0:T(8,128)}, f32[1280,1024]{1,0:T(8,128)}, f32[1280,1024]{1,0:T(8,128)}) fusion(f32[160,8,8,128]{3,2,1,0:T(8,128)S(1)} %bitcast.70, f32[1280,1024]{1,0:T(8,128)} %param.28, bf16[128,1280]{1,0:T(8,128)(2,1)S(1)} %all_gather.9, f32[128,1024]{1,0:T(8,128)S(1)} %copy-done.13, f32[128,1024]{1,0:T(8,128)S(1)} %copy-done.7, ...), kind=kOutput, calls=%fused_computation.10 | convolution fusion | flops 349437952 | bytes 32833536 | tf_op jit(solution)/shard_map/dot_general | solution.py:46
  (70 shorter events, 17.7 us)
Async XLA Ops:
  7.2 115.9 %copy-start = (bf16[1024,1280]{1,0:T(8,128)(2,1)S(1)}, bf16[1024,1280]{1,0:T(8,128)(2,1)}, u32[]{:S(2)}) copy-start(bf16[1024,1280]{1,0:T(8,128)(2,1)} %param.20) | copy-start | bytes 7864324
  7.2 113.9 %all-reduce.7.cloned.1.call-start = ((), (), s32[]{:S(2)}) async-start(), calls=%async_computation.3 | async-start | bytes 4194304 | tf_op jit(solution)/shard_map/psum | solution.py:80
  14.7 19.0 %copy-start.4 = (bf16[1280,1024]{1,0:T(8,128)(2,1)S(1)}, bf16[1280,1024]{1,0:T(8,128)(2,1)}, u32[]{:S(2)}) copy-start(bf16[1280,1024]{1,0:T(8,128)(2,1)} %param.21) | copy-start | bytes 7864324
  27.4 7.6 %copy-start.11 = (bf16[1280,1024]{1,0:T(8,128)(2,1)S(1)}, bf16[1280,1024]{1,0:T(8,128)(2,1)}, u32[]{:S(2)}) copy-start(bf16[1280,1024]{1,0:T(8,128)(2,1)} %param.18) | copy-start | bytes 7864324
  36.3 127.6 %reduce-scatter.2.cloned.1.call-start = ((), (), s32[]{:S(2)}) async-start(), calls=%async_computation.1 | async-start | bytes 1474560 | tf_op jit(solution)/shard_map/reduce_scatter | solution.py:94
  121.1 3.0 copy-start.2
  123.1 1.6 copy-start.9
  123.6 40.2 %copy-start.15 = (bf16[16,1280]{1,0:T(8,128)(2,1)S(1)}, bf16[16,1280]{1,0:T(8,128)(2,1)}, u32[]{:S(2)}) copy-start(bf16[16,1280]{1,0:T(8,128)(2,1)} %param.15) | copy-start | bytes 122884
  125.9 149.5 %all-reduce.5.cloned.1.call-start = ((), (), s32[]{:S(2)}) async-start(), calls=%async_computation.2 | async-start | bytes 2097152 | tf_op jit(solution)/shard_map/psum | solution.py:107
  175.8 16.3 %copy-start.3 = (bf16[1024,1280]{1,0:T(8,128)(2,1)S(1)}, bf16[1024,1280]{1,0:T(8,128)(2,1)}, u32[]{:S(2)}) copy-start(bf16[1024,1280]{1,0:T(8,128)(2,1)} %param.23) | copy-start | bytes 7864324
  190.4 0.7 copy-start.10
  225.4 50.1 %copy-start.5 = (bf16[1280,1024]{1,0:T(8,128)(2,1)S(1)}, bf16[1280,1024]{1,0:T(8,128)(2,1)}, u32[]{:S(2)}) copy-start(bf16[1280,1024]{1,0:T(8,128)(2,1)} %param.21) | copy-start | bytes 7864324
  275.4 3.1 copy-start.6
  275.4 3.1 copy-start.7
  275.4 3.1 copy-start.8
  275.5 3.1 copy-start.13
  275.5 3.2 %copy-start.14 = (f32[128,1024]{1,0:T(8,128)S(1)}, f32[128,1024]{1,0:T(8,128)}, u32[]{:S(2)}) copy-start(f32[128,1024]{1,0:T(8,128)} %get-tuple-element.10) | copy-start | bytes 1572868
  281.4 2.2 slice-start
  281.4 3.5 %slice-start.2 = ((s8[5242880]{0:T(1024)(128)(4,1)}), s8[4194304]{0:T(1024)(128)(4,1)S(1)}, s32[]{:S(2)}) async-start(s8[5242880]{0:T(1024)(128)(4,1)} %bitcast.74), calls=%async_computation.6 | async-start | bytes 8388608
  282.7 2.4 copy-start.12
  282.7 2.7 slice-start.1
  282.7 3.0 slice-start.3
  293.5 10.1 %copy-start.1 = (bf16[1024,1280]{1,0:T(8,128)(2,1)S(1)}, bf16[1024,1280]{1,0:T(8,128)(2,1)}, u32[]{:S(2)}) copy-start(bf16[1024,1280]{1,0:T(8,128)(2,1)} %param.20) | copy-start | bytes 7864324
Sparse Core Ops, SparseCore 0:
  36.4 84.6 all-reduce.6
  126.0 37.7 reduce-scatter.1
  225.5 49.9 all-reduce.4
where the time goes:
time: 314 us; the launch traced here: 310 us
  waiting for transfers between devices  162 us (52%)
  matrix products  58.2 us (19%)
  blocking collectives  36.7 us (12%)
  local copies, waits for them, and re-layouts  29.3 us (9%)
  between operations  14 us (4%)
  other arithmetic  9.82 us (3%)
    psum x1, waiting for transfers between devices, shards(): lax.psum((matmul(normed, w_gate), matmul(normed, w_up), matmul(normed, pr...  84.8 us
    dot_general x7, matrix products, inner_left(): lax.dot_general(left, right, (((0,), (0,)), ((), ())), preferred_element_...  43.3 us
    psum x1, waiting for transfers between devices, shards(): lax.psum((inner_right(error, w_down), inner_right(error_tan, w_down) + in...  39.3 us
    reduce_scatter x1, waiting for transfers between devices, shards(): lax.psum_scatter(jnp.concatenate([primal, tangent], axis=1), ('row', 'dep...  37.9 us
    unnamed x44, local copies, waits for them, and re-layouts  15.4 us
    all_gather x1, blocking collectives, shards(): normed = lax.all_gather(normed_rows, ('row', 'depth'), axis=0, tiled=True)  11.7 us
    dot_general x7, matrix products, matmul(): return jnp.dot(left, right, preferred_element_type=jnp.float32)  10.4 us
    all_gather x1, blocking collectives, shards(): lax.all_gather(tangent_rows, ('row', 'depth'), axis=0, tiled=True)  9.39 us
  transfers between devices with their start and end apart: 3, of which 3 were waited for; matrix products, arithmetic and copies ran while one was open for 3% of the time, Pallas kernels for 0%

commit v1 on v0

v1 whole, which is shorter than its diff:
```python
import functools

import jax
import jax.numpy as jnp
from jax import lax
from jax.experimental import pallas as pl
from jax.experimental.pallas import tpu as pltpu
from jax.sharding import PartitionSpec as P

TILE = 128
STEP = 1000

beta_one = 0.9
beta_two = 0.999
adam_floor = 1e-08
norm_floor = 1e-05

F32 = jnp.float32
BF16 = jnp.bfloat16
MESH = pl.DeviceIdType.MESH


def dot(left, right, dims):
    return lax.dot_general(left, right, ((dims[:1], dims[1:]), ((), ())), preferred_element_type=F32)


def exchange(
    n_row, n_col, n_depth,
    x_ref, t_ref, gain_ref, w_gate, w_up, w_down, p_gate, p_up, p_down,
    normed_ref, hid_ref, err_ref, back_ref,
    front, down, x_all, xg, sq_send, sq_recv, scale_all,
    part, part_in, coef, out_part, out_in, bk_part, bk_in,
    load_sem, x_s, x_r, sq_s, sq_r, sc_s, sc_r, part_s, part_r, hid_s, hid_r,
    out_s, out_r, err_s, err_r, bk_s, bk_r, back_s, back_r,
):
    n_group = n_row * n_depth
    row, c, depth = lax.axis_index("row"), lax.axis_index("col"), lax.axis_index("depth")
    g = row * n_depth + depth
    tokens, width = normed_ref.shape
    features = width * n_col
    hidden = w_gate.shape[1]
    tile_f, tile_d = min(256, hidden), min(256, width)

    loads = [
        pltpu.make_async_copy(src, dst, load_sem.at[i])
        for i, (src, dst) in enumerate([
            (w_gate, front.at[0]), (w_up, front.at[1]), (p_gate, front.at[2]), (p_up, front.at[3]),
            (w_down, down.at[0]), (p_down, down.at[1]),
        ])
    ]
    for load in loads:
        load.start()

    def group_id(k):
        to = lax.rem(g + k, n_group)
        return to, {"row": lax.div(to, n_depth), "depth": lax.rem(to, n_depth)}

    def col_id(k):
        to = lax.rem(c + k, n_col)
        return to, {"col": to}

    def remote(src, dst, send, recv, where):
        return pltpu.make_async_remote_copy(
            src_ref=src, dst_ref=dst, send_sem=send, recv_sem=recv, device_id=where, device_id_type=MESH
        )

    def group_loop(body):
        lax.fori_loop(1, n_group, lambda k, carry: (body(k), carry)[1], 0)

    barrier = pltpu.get_barrier_semaphore()

    def greet(k):
        pl.semaphore_signal(barrier, inc=1, device_id=group_id(k)[1], device_id_type=MESH)

    group_loop(greet)
    for k in range(1, n_col):
        pl.semaphore_signal(barrier, inc=1, device_id=col_id(k)[1], device_id_type=MESH)
    pl.semaphore_wait(barrier, n_group + n_col - 2)

    def x_copy(k):
        return remote(x_ref, x_all.at[g], x_s.at[k], x_r.at[k], group_id(k)[1])

    def sq_copy(k):
        to, where = col_id(k)
        return remote(sq_send.at[to], sq_recv.at[c], sq_s.at[k], sq_r.at[k], where)

    def sc_copy(k):
        return remote(scale_all.at[c], scale_all.at[c], sc_s.at[k], sc_r.at[k], col_id(k)[1])

    def part_copy(a, k):
        to, where = col_id(k)
        return remote(part.at[a, to], part_in.at[a, c], part_s.at[a, k], part_r.at[a, k], where)

    def hid_copy(a, k):
        return remote(hid_ref.at[a, c], hid_ref.at[a, c], hid_s.at[a, k], hid_r.at[a, k], col_id(k)[1])

    def out_copy(a, k):
        to, where = group_id(k)
        return remote(out_part.at[a, to], out_in.at[a, g], out_s.at[a, k], out_r.at[a, k], where)

    def err_copy(a, k):
        return remote(err_ref.at[a, g], err_ref.at[a, g], err_s.at[a, k], err_r.at[a, k], group_id(k)[1])

    def bk_copy(a, k):
        to, where = col_id(k)
        return remote(bk_part.at[a, to], bk_in.at[a, c], bk_s.at[a, k], bk_r.at[a, k], where)

    def back_copy(a, k):
        return remote(back_ref.at[a, c], back_ref.at[a, c], back_s.at[a, k], back_r.at[a, k], col_id(k)[1])

    def col_each(act, *at):
        for k in range(1, n_col):
            act(*at, k)

    group_loop(lambda k: x_copy(k).start())
    x_all[g] = x_ref[...]
    group_loop(lambda k: x_copy(k).wait_recv())
    feats = x_all[...].reshape(tokens, width).astype(F32)
    squares = jnp.sum(feats * feats, axis=1, keepdims=True)
    sq_send[...] = jnp.broadcast_to(squares, (tokens, 128)).reshape(sq_send.shape)
    col_each(lambda k: sq_copy(k).start())
    xg[...] = (feats * gain_ref[...]).astype(BF16)

    for a in range(4):
        loads[a].wait()

        @pl.loop(0, hidden // tile_f)
        def _(j):
            cols = pl.ds(pl.multiple_of(j * tile_f, tile_f), tile_f)
            value = dot(xg[...], front[a, :, cols], (1, 0))
            part[a, :, :, cols] = value.astype(BF16).reshape(n_col, tokens // n_col, tile_f)

        col_each(lambda a, k: part_copy(a, k).start(), a)

    total = sq_send[c]
    for k in range(1, n_col):
        sq_copy(k).wait_recv()
        total = total + sq_recv[lax.rem(c - k + n_col, n_col)]
    scale = lax.rsqrt(total / features + norm_floor)
    scale_all[c] = scale
    col_each(lambda k: sc_copy(k).start())

    def summed(own, came, copy, a):
        value = own[a, c].astype(F32)
        for k in range(1, n_col):
            copy(a, k).wait_recv()
            value = value + came[a, lax.rem(c - k + n_col, n_col)].astype(F32)
        return value

    scale = scale[:, :1]
    gate_pre = summed(part, part_in, part_copy, 0) * scale
    sig = jax.nn.sigmoid(gate_pre)
    act = gate_pre * sig
    slope = sig * (1.0 + gate_pre * (1.0 - sig))
    bend = sig * (1.0 - sig) * (2.0 + gate_pre * (1.0 - 2.0 * sig))
    coef[0] = act
    coef[1] = slope
    coef[2] = bend
    up_pre = summed(part, part_in, part_copy, 1) * scale
    hid_ref[0, c] = (coef[0] * up_pre).astype(BF16)
    col_each(lambda a, k: hid_copy(a, k).start(), 0)
    coef[3] = up_pre
    gate_tan = summed(part, part_in, part_copy, 2) * scale
    coef[4] = gate_tan
    up_tan = summed(part, part_in, part_copy, 3) * scale
    hid_ref[1, c] = (coef[1] * coef[4] * coef[3] + coef[0] * up_tan).astype(BF16)
    col_each(lambda a, k: hid_copy(a, k).start(), 1)
    coef[2] = up_tan * coef[1] + coef[3] * coef[2] * coef[4]
    coef[4] = coef[1] * coef[4]
    coef[1] = coef[3] * coef[1]

    def down_product(a, make):
        @pl.loop(0, width // tile_d)
        def _(j):
            cols = pl.ds(pl.multiple_of(j * tile_d, tile_d), tile_d)
            out_part[a, :, :, cols] = make(cols).astype(BF16).reshape(n_group, tokens // n_group, tile_d)

        group_loop(lambda k: out_copy(a, k).start())

    def flat(ref, a):
        value = ref[a]
        return value.reshape(tokens, value.shape[-1])

    loads[4].wait()
    loads[5].wait()
    col_each(lambda a, k: hid_copy(a, k).wait_recv(), 0)
    down_product(0, lambda cols: dot(flat(hid_ref, 0), down[0, :, cols], (1, 0)))
    col_each(lambda a, k: hid_copy(a, k).wait_recv(), 1)
    down_product(
        1,
        lambda cols: dot(flat(hid_ref, 1), down[0, :, cols], (1, 0))
        + dot(flat(hid_ref, 0), down[1, :, cols], (1, 0)),
    )

    def owner_sum(a, start):
        def add(k, value):
            out_copy(a, k).wait_recv()
            return value + out_in[a, lax.rem(g - k + n_group, n_group)].astype(F32)

        return lax.fori_loop(1, n_group, add, start + out_part[a, g].astype(F32))

    outputs = owner_sum(0, x_ref[...].astype(F32))
    err_ref[0, g] = (outputs - t_ref[...].astype(F32)).astype(BF16)
    group_loop(lambda k: err_copy(0, k).start())
    err_ref[1, g] = owner_sum(1, jnp.zeros(x_ref.shape, F32)).astype(BF16)
    group_loop(lambda k: err_copy(1, k).start())

    col_each(lambda k: sc_copy(k).wait_recv())
    scales = scale_all[...].reshape(tokens, 128)[:, :1]
    feats = x_all[...].reshape(tokens, width).astype(F32)
    normed_ref[...] = (feats * scales * gain_ref[...]).astype(BF16)

    def back_product(a, make):
        @pl.loop(0, hidden // tile_f)
        def _(j):
            rows = pl.ds(pl.multiple_of(j * tile_f, tile_f), tile_f)
            bk_part[a, :, :, rows] = make(rows).astype(BF16).reshape(n_col, tokens // n_col, tile_f)

        col_each(lambda a, k: bk_copy(a, k).start(), a)

    group_loop(lambda k: err_copy(0, k).wait_recv())
    back_product(0, lambda rows: dot(flat(err_ref, 0), down[0, rows, :], (1, 1)))
    group_loop(lambda k: err_copy(1, k).wait_recv())
    back_product(
        1,
        lambda rows: dot(flat(err_ref, 1), down[0, rows, :], (1, 1))
        + dot(flat(err_ref, 0), down[1, rows, :], (1, 1)),
    )

    back_hidden = summed(bk_part, bk_in, bk_copy, 0)
    back_ref[0, c] = (back_hidden * coef[1]).astype(BF16)
    col_each(lambda a, k: back_copy(a, k).start(), 0)
    back_ref[1, c] = (back_hidden * coef[0]).astype(BF16)
    col_each(lambda a, k: back_copy(a, k).start(), 1)
    back_tan = summed(bk_part, bk_in, bk_copy, 1)
    back_ref[2, c] = (back_tan * coef[1] + back_hidden * coef[2]).astype(BF16)
    col_each(lambda a, k: back_copy(a, k).start(), 2)
    back_ref[3, c] = (back_tan * coef[0] + back_hidden * coef[4]).astype(BF16)
    col_each(lambda a, k: back_copy(a, k).start(), 3)

    for a in range(4):
        col_each(lambda a, k: back_copy(a, k).wait_recv(), a)

    def sent(k):
        x_copy(k).wait_send()
        for a in range(2):
            out_copy(a, k).wait_send()
            err_copy(a, k).wait_send()

    group_loop(sent)
    for k in range(1, n_col):
        sq_copy(k).wait_send()
        sc_copy(k).wait_send()
        for a in range(4):
            part_copy(a, k).wait_send()
            back_copy(a, k).wait_send()
        for a in range(2):
            hid_copy(a, k).wait_send()
            bk_copy(a, k).wait_send()


def run_exchange(mesh, x, t, gain, w_gate, w_up, w_down, p_gate, p_up, p_down):
    n_row, n_col, n_depth = mesh.shape["row"], mesh.shape["col"], mesh.shape["depth"]
    n_group = n_row * n_depth
    rows, width = x.shape
    hidden = w_gate.shape[1]
    tokens = rows * n_group
    run = tokens // n_col
    vmem = pl.BlockSpec(memory_space=pltpu.VMEM)
    hbm = pl.BlockSpec(memory_space=pl.ANY)
    sem = pltpu.SemaphoreType.DMA
    pair = lambda *shape: [sem(shape), sem(shape)]
    shape = jax.ShapeDtypeStruct
    return pl.pallas_call(
        functools.partial(exchange, n_row, n_col, n_depth),
        out_shape=(
            shape((tokens, width), BF16),
            shape((2, n_col, run, hidden), BF16),
            shape((2, n_group, rows, width), BF16),
            shape((4, n_col, run, hidden), BF16),
        ),
        in_specs=[vmem] * 3 + [hbm] * 6,
        out_specs=(vmem,) * 4,
        scratch_shapes=[
            pltpu.VMEM((4, width, hidden), BF16),
            pltpu.VMEM((2, hidden, width), BF16),
            pltpu.VMEM((n_group, rows, width), BF16),
            pltpu.VMEM((tokens, width), BF16),
            pltpu.VMEM((n_col, run, 128), F32),
            pltpu.VMEM((n_col, run, 128), F32),
            pltpu.VMEM((n_col, run, 128), F32),
            pltpu.VMEM((4, n_col, run, hidden), BF16),
            pltpu.VMEM((4, n_col, run, hidden), BF16),
            pltpu.VMEM((5, run, hidden), F32),
            pltpu.VMEM((2, n_group, rows, width), BF16),
            pltpu.VMEM((2, n_group, rows, width), BF16),
            pltpu.VMEM((2, n_col, run, hidden), BF16),
            pltpu.VMEM((2, n_col, run, hidden), BF16),
            sem((6,)),
            *pair(n_group), *pair(n_col), *pair(n_col), *pair(4, n_col), *pair(2, n_col),
            *pair(2, n_group), *pair(2, n_group), *pair(2, n_col), *pair(4, n_col),
        ],
        compiler_params=pltpu.CompilerParams(
            collective_id=0, has_side_effects=True, vmem_limit_bytes=56 * 2**20
        ),
    )(x, t, gain.reshape(1, width), w_gate, w_up, w_down, p_gate, p_up, p_down)


def update_tile(moment, second, probe, grad, curve, new_moment, new_second, step, cols):
    product = probe[:, cols].astype(F32) * curve
    average = jnp.sum(product) * (1.0 / (TILE * TILE))
    moved = beta_one * moment[:, cols] + (1.0 - beta_one) * grad
    square = beta_two * second[:, cols] + (1.0 - beta_two) * average * average
    new_moment[:, cols] = moved
    new_second[:, cols] = square
    root = jnp.sqrt(square * (1.0 / (1.0 - beta_two**STEP)))
    step[:, cols] = moved * (1.0 / (1.0 - beta_one**STEP)) / (root + adam_floor)


def update_front(normed, back, moment, second, probe, new_moment, new_second, step):
    tokens = normed.shape[0]
    left = normed[...].T
    breadth = moment.shape[1]
    for j in range(breadth // TILE):
        cols = slice(j * TILE, (j + 1) * TILE)
        grad = dot(left, back[0, 0, :, :, cols].reshape(tokens, TILE), (1, 0))
        curve = dot(left, back[1, 0, :, :, cols].reshape(tokens, TILE), (1, 0))
        update_tile(moment, second, probe, grad, curve, new_moment, new_second, step, cols)


def update_down(hid, err, moment, second, probe, new_moment, new_second, step):
    tokens = err.shape[1] * err.shape[2]
    primal = hid[0].reshape(tokens, TILE).T
    tangent = hid[1].reshape(tokens, TILE).T
    breadth = moment.shape[1]
    for j in range(breadth // TILE):
        cols = slice(j * TILE, (j + 1) * TILE)
        error = err[0, :, :, cols].reshape(tokens, TILE)
        error_tan = err[1, :, :, cols].reshape(tokens, TILE)
        grad = dot(primal, error, (1, 0))
        curve = dot(tangent, error, (1, 0)) + dot(primal, error_tan, (1, 0))
        update_tile(moment, second, probe, grad, curve, new_moment, new_second, step, cols)


def run_update(body, acts, act_specs, moment, second, probe):
    height, breadth = moment.shape
    block = pl.BlockSpec((TILE, breadth), lambda i: (i, 0))
    return pl.pallas_call(
        body,
        grid=(height // TILE,),
        out_shape=(jax.ShapeDtypeStruct(moment.shape, F32),) * 3,
        in_specs=[*act_specs, block, block, block],
        out_specs=(block,) * 3,
        compiler_params=pltpu.CompilerParams(
            dimension_semantics=("arbitrary",), vmem_limit_bytes=40 * 2**20
        ),
    )(*acts, moment, second, probe)


def shards(
    mesh, inputs, targets, norm_gain, w_gate, w_up, w_down, probe_gate, probe_up, probe_down,
    moment_gate, moment_up, moment_down, second_gate, second_up, second_down,
):
    normed, hid, err, back = run_exchange(
        mesh, inputs, targets, norm_gain, w_gate, w_up, w_down, probe_gate, probe_up, probe_down
    )
    tokens = normed.shape[0]
    _, n_col, run, hidden = back.shape
    pairs = back.reshape(2, 2, n_col, run, hidden)
    normed_spec = pl.BlockSpec((tokens, TILE), lambda i: (0, i))

    def back_spec(which):
        return pl.BlockSpec((2, 1, n_col, run, hidden), lambda i: (0, which, 0, 0, 0))

    gate = run_update(
        update_front, (normed, pairs), (normed_spec, back_spec(0)), moment_gate, second_gate, probe_gate
    )
    up = run_update(
        update_front, (normed, pairs), (normed_spec, back_spec(1)), moment_up, second_up, probe_up
    )
    down = run_update(
        update_down,
        (hid, err),
        (
            pl.BlockSpec((2, n_col, run, TILE), lambda i: (0, 0, 0, i)),
            pl.BlockSpec(err.shape, lambda i: (0, 0, 0, 0)),
        ),
        moment_down, second_down, probe_down,
    )
    return (gate[0], up[0], down[0], gate[1], up[1], down[1], gate[2], up[2], down[2])


def solution(mesh):
    group = ("row", "depth")
    rows, cols = P(group, "col"), P("col", group)
    return jax.shard_map(
        functools.partial(shards, mesh),
        mesh=mesh,
        in_specs=(rows, rows, P("col"), cols, cols, rows) + (cols, cols, rows) * 3,
        out_specs=(cols, cols, rows) * 3,
        check_vma=False,
    )
```

time: 314 us -> 141 us (0.45); the launches traced: 310 us -> 141 us
  waiting for transfers between devices: 162 us -> 0 us
  Pallas kernels: 0 us -> 127 us
  matrix products: 58.2 us -> 0 us
  blocking collectives: 36.7 us -> 0 us
  local copies, waits for them, and re-layouts: 29.3 us -> 13.4 us
  between operations: 14 us -> 0.7 us
  other arithmetic: 9.82 us -> 0 us
    pallas_call x0 -> x4, Pallas kernels: none -> 127 us  [the longest x1 99.2 us: run_exchange(): pl.pallas_call(functools.partial(exchange, n_row, n_col, n_depth), out_sh...]
    psum x2 -> x0, waiting for transfers between devices: 124 us -> none  [the longest x1 84.8 us: shards(): lax.psum((matmul(normed, w_gate), matmul(normed, w_up), matmul(normed, pr...]
    dot_general x17 -> x0, matrix products: 58.2 us -> none  [the longest x7 43.3 us: inner_left(): lax.dot_general(left, right, (((0,), (0,)), ((), ())), preferred_element_...]
    reduce_scatter x1 -> x0, waiting for transfers between devices: 37.9 us -> none  [shards(): lax.psum_scatter(jnp.concatenate([primal, tangent], axis=1), ('row', 'dep...]
    all_gather x3 -> x0, blocking collectives: 30.4 us -> none  [the longest x1 11.7 us: shards(): normed = lax.all_gather(normed_rows, ('row', 'depth'), axis=0, tiled=True)]
    psum x1 -> x0, blocking collectives: 6.38 us -> none  [shards(): squares = lax.psum(jnp.sum(feats * feats, axis=1), 'col')]
    mul x1 -> x0, local copies, waits for them, and re-layouts: 5.88 us -> none  [adahessian(): averaged = tile_means(probe.astype(jnp.float32) * curvature)]
    reduce_sum x4 -> x0, other arithmetic: 4.74 us -> none  [the longest x3 3.69 us: tile_means(): means = jnp.mean(blocks, axis=(1, 3), keepdims=True)]
  transfers between devices with their start and end apart: 3 -> 0, of which waited for: 3 -> 0; matrix products, arithmetic and copies ran while one was open for 3% -> 0% of each run, Pallas kernels for 0% -> 0%
where the time goes in v1:
time: 141 us
  Pallas kernels  127 us (90%)
  local copies, waits for them, and re-layouts  13.4 us (10%)
    pallas_call x1, Pallas kernels, run_exchange(): pl.pallas_call(functools.partial(exchange, n_row, n_col, n_depth), out_sh...  99.2 us
    pallas_call x3, Pallas kernels, run_update(): pl.pallas_call(body, grid=(height // TILE,), out_shape=(jax.ShapeDtypeStr...  27.5 us
    unnamed x26, local copies, waits for them, and re-layouts  12.2 us

profile of v1, /device:TPU:29, one launch (start us, length us, event | category | flops | bytes accessed | tf_op | source)
XLA Modules:
  0.0 140.8 jit_solution(4838246133374355100)
XLA Ops:
  0.6 1.3 reshape.24.gain_ref
  1.9 0.0 copy-start
  1.9 0.0 copy-start.3
  1.9 99.2 %shard_map.214 = (bf16[128,1280]{1,0:T(8,128)(2,1)}, bf16[2,4,32,1024]{3,2,1,0:T(8,128)(2,1)}, bf16[2,8,16,1280]{3,2,1,0:T(8,128)(2,1)}, bf16[4,4,32,1024]{3,2,1,0:T(8,128)(2,1)}) custom-call(bf16[16,1280]{1,0:T(8,128)(2,1)} %x_ref.1, bf16[16,1280]{1,0:T(8,128)(2,1)} %t_ref.1, f32[1,1280]{1,0:T(1,128)} %reshape.24.gain_ref, bf16[1280,1024]{1,0:T(8,128)(2,1)} %w_gate.1, ...), custom_call_target="tpu_custom_call" | custom-call | tf_op jit(solution)/shard_map/pallas_call | solution.py:274
  101.1 0.0 copy-done
  101.2 0.0 copy-done.3
  101.2 0.0 copy-start.4
  101.2 2.5 %copy-done.4 = f32[1280,1024]{1,0:T(8,128)S(1)} copy-done((f32[1280,1024]{1,0:T(8,128)S(1)}, f32[1280,1024]{1,0:T(8,128)}, u32[]{:S(2)}) %copy-start.4) | copy-done | bytes 5242904
  103.7 0.0 copy-start.9
  103.7 1.2 copy-done.9
  104.9 0.0 copy-start.10
  104.9 1.0 copy-done.10
  105.9 9.4 %shard_map.216 = (f32[1280,1024]{1,0:T(8,128)}, f32[1280,1024]{1,0:T(8,128)}, f32[1280,1024]{1,0:T(8,128)}) custom-call(bf16[128,1280]{1,0:T(8,128)(2,1)S(1)} %copy-done.10, bf16[2,2,4,32,1024]{4,3,2,1,0:T(8,128)(2,1)S(1)} %bitcast.1, f32[1280,1024]{1,0:T(8,128)S(1)} %copy-done.3, f32[1280,1024]{1,0:T(8,128)S(1)} %copy-done.4, bf16[1280,1024]{1,0:T(8,128)(2,1)S(1)} %copy-done), custom_call_target="tpu_custom_call" | custom-call | tf_op jit(solution)/shard_map/pallas_call | solution.py:348
  115.3 0.0 copy-done.1
  115.3 0.0 copy-done.6
  115.3 2.5 %copy-done.5 = f32[1280,1024]{1,0:T(8,128)S(1)} copy-done((f32[1280,1024]{1,0:T(8,128)S(1)}, f32[1280,1024]{1,0:T(8,128)}, u32[]{:S(2)}) %copy-start.5) | copy-done | bytes 5242904
  117.8 9.4 %shard_map.215 = (f32[1280,1024]{1,0:T(8,128)}, f32[1280,1024]{1,0:T(8,128)}, f32[1280,1024]{1,0:T(8,128)}) custom-call(bf16[128,1280]{1,0:T(8,128)(2,1)S(1)} %copy-done.10, bf16[2,2,4,32,1024]{4,3,2,1,0:T(8,128)(2,1)S(1)} %bitcast.2, f32[1280,1024]{1,0:T(8,128)S(1)} %copy-done.5, f32[1280,1024]{1,0:T(8,128)S(1)} %copy-done.6, bf16[1280,1024]{1,0:T(8,128)(2,1)S(1)} %copy-done.1), custom_call_target="tpu_custom_call" | custom-call | tf_op jit(solution)/shard_map/pallas_call | solution.py:348
  127.2 0.0 copy-done.2
  127.2 0.0 copy-done.11
  127.2 0.0 copy-done.12
  127.2 0.0 copy-start.7
  127.2 2.5 %copy-done.7 = f32[1024,1280]{1,0:T(8,128)S(1)} copy-done((f32[1024,1280]{1,0:T(8,128)S(1)}, f32[1024,1280]{1,0:T(8,128)}, u32[]{:S(2)}) %copy-start.7) | copy-done | bytes 5242904
  129.7 2.5 %copy-done.8 = f32[1024,1280]{1,0:T(8,128)S(1)} copy-done((f32[1024,1280]{1,0:T(8,128)S(1)}, f32[1024,1280]{1,0:T(8,128)}, u32[]{:S(2)}) %copy-start.8) | copy-done | bytes 5242904
  132.2 8.7 %shard_map.217 = (f32[1024,1280]{1,0:T(8,128)}, f32[1024,1280]{1,0:T(8,128)}, f32[1024,1280]{1,0:T(8,128)}) custom-call(bf16[2,4,32,1024]{3,2,1,0:T(8,128)(2,1)S(1)} %copy-done.12, bf16[2,8,16,1280]{3,2,1,0:T(8,128)(2,1)S(1)} %copy-done.11, f32[1024,1280]{1,0:T(8,128)S(1)} %copy-done.7, f32[1024,1280]{1,0:T(8,128)S(1)} %copy-done.8, ...), custom_call_target="tpu_custom_call" | custom-call | tf_op jit(solution)/shard_map/pallas_call | solution.py:348
  (7 shorter events, 0.0 us)
Async XLA Ops:
  1.9 99.2 %copy-start = (bf16[1280,1024]{1,0:T(8,128)(2,1)S(1)}, bf16[1280,1024]{1,0:T(8,128)(2,1)}, u32[]{:S(2)}) copy-start(bf16[1280,1024]{1,0:T(8,128)(2,1)} %probe.4) | copy-start | bytes 7864324
  1.9 99.2 %copy-start.3 = (f32[1280,1024]{1,0:T(8,128)S(1)}, f32[1280,1024]{1,0:T(8,128)}, u32[]{:S(2)}) copy-start(f32[1280,1024]{1,0:T(8,128)} %moment.4) | copy-start | bytes 15728644
  101.2 2.5 %copy-start.4 = (f32[1280,1024]{1,0:T(8,128)S(1)}, f32[1280,1024]{1,0:T(8,128)}, u32[]{:S(2)}) copy-start(f32[1280,1024]{1,0:T(8,128)} %second.4) | copy-start | bytes 15728644
  103.7 1.2 copy-start.9
  104.9 1.0 copy-start.10
  105.9 9.4 %copy-start.1 = (bf16[1280,1024]{1,0:T(8,128)(2,1)S(1)}, bf16[1280,1024]{1,0:T(8,128)(2,1)}, u32[]{:S(2)}) copy-start(bf16[1280,1024]{1,0:T(8,128)(2,1)} %probe.3) | copy-start | bytes 7864324
  105.9 9.4 %copy-start.6 = (f32[1280,1024]{1,0:T(8,128)S(1)}, f32[1280,1024]{1,0:T(8,128)}, u32[]{:S(2)}) copy-start(f32[1280,1024]{1,0:T(8,128)} %second.3) | copy-start | bytes 15728644
  115.3 2.5 %copy-start.5 = (f32[1280,1024]{1,0:T(8,128)S(1)}, f32[1280,1024]{1,0:T(8,128)}, u32[]{:S(2)}) copy-start(f32[1280,1024]{1,0:T(8,128)} %moment.3) | copy-start | bytes 15728644
  117.8 9.4 %copy-start.2 = (bf16[1024,1280]{1,0:T(8,128)(2,1)S(1)}, bf16[1024,1280]{1,0:T(8,128)(2,1)}, u32[]{:S(2)}) copy-start(bf16[1024,1280]{1,0:T(8,128)(2,1)} %probe.5) | copy-start | bytes 7864324
  117.8 9.4 %copy-start.11 = (bf16[2,8,16,1280]{3,2,1,0:T(8,128)(2,1)S(1)}, bf16[2,8,16,1280]{3,2,1,0:T(8,128)(2,1)}, u32[]{:S(2)}) copy-start(bf16[2,8,16,1280]{3,2,1,0:T(8,128)(2,1)} %get-tuple-element.27.err) | copy-start | bytes 1966084
  117.8 9.4 %copy-start.12 = (bf16[2,4,32,1024]{3,2,1,0:T(8,128)(2,1)S(1)}, bf16[2,4,32,1024]{3,2,1,0:T(8,128)(2,1)}, u32[]{:S(2)}) copy-start(bf16[2,4,32,1024]{3,2,1,0:T(8,128)(2,1)} %get-tuple-element.26.hid) | copy-start | bytes 1572868
  127.2 2.5 %copy-start.7 = (f32[1024,1280]{1,0:T(8,128)S(1)}, f32[1024,1280]{1,0:T(8,128)}, u32[]{:S(2)}) copy-start(f32[1024,1280]{1,0:T(8,128)} %moment.5) | copy-start | bytes 15728644
  129.7 2.5 %copy-start.8 = (f32[1024,1280]{1,0:T(8,128)S(1)}, f32[1024,1280]{1,0:T(8,128)}, u32[]{:S(2)}) copy-start(f32[1024,1280]{1,0:T(8,128)} %second.5) | copy-start | bytes 15728644

commit v2 on v1

--- a/solution.py
+++ b/solution.py
@@ -1,4 +1,5 @@
 import functools
+import math
 
 import jax
 import jax.numpy as jnp
@@ -24,19 +25,34 @@
     return lax.dot_general(left, right, ((dims[:1], dims[1:]), ((), ())), preferred_element_type=F32)
 
 
+def update(moment, second, probe, grad, curve):
+    product = jnp.sum(probe.astype(F32) * curve, axis=0, keepdims=True)
+    parts = []
+    for j in range(second.shape[1] // TILE):
+        cols = slice(j * TILE, (j + 1) * TILE)
+        average = jnp.sum(product[:, cols], axis=1, keepdims=True) * (1.0 / (TILE * TILE))
+        parts.append(beta_two * second[:, cols] + (1.0 - beta_two) * average * average)
+    square = jnp.concatenate(parts, axis=1) if len(parts) > 1 else parts[0]
+    moved = beta_one * moment + (1.0 - beta_one) * grad
+    scaled = square * (1.0 / (1.0 - beta_two**STEP))
+    root = scaled * lax.rsqrt(scaled)
+    return moved, square, moved * (1.0 / (1.0 - beta_one**STEP)) / (root + adam_floor)
+
+
 def exchange(
     n_row, n_col, n_depth,
     x_ref, t_ref, gain_ref, w_gate, w_up, w_down, p_gate, p_up, p_down,
-    normed_ref, hid_ref, err_ref, back_ref,
-    front, down, x_all, xg, sq_send, sq_recv, scale_all,
+    m_gate, m_up, m_down, s_gate, s_up, s_down,
+    normed_ref, back_ref, probes, moments, seconds, new_moment, new_second, step,
+    hid_ref, err_ref, front, down, x_all, xg, sq_send, sq_recv, scale_all,
     part, part_in, coef, out_part, out_in, bk_part, bk_in,
-    load_sem, x_s, x_r, sq_s, sq_r, sc_s, sc_r, part_s, part_r, hid_s, hid_r,
+    load_sem, state_sem, x_s, x_r, sq_s, sq_r, sc_s, sc_r, part_s, part_r, hid_s, hid_r,
     out_s, out_r, err_s, err_r, bk_s, bk_r, back_s, back_r,
 ):
     n_group = n_row * n_depth
     row, c, depth = lax.axis_index("row"), lax.axis_index("col"), lax.axis_index("depth")
     g = row * n_depth + depth
-    tokens, width = normed_ref.shape
+    width, tokens = normed_ref.shape
     features = width * n_col
     hidden = w_gate.shape[1]
     tile_f, tile_d = min(256, hidden), min(256, width)
@@ -44,8 +60,15 @@
     loads = [
         pltpu.make_async_copy(src, dst, load_sem.at[i])
         for i, (src, dst) in enumerate([
-            (w_gate, front.at[0]), (w_up, front.at[1]), (p_gate, front.at[2]), (p_up, front.at[3]),
+            (w_gate, front.at[0]), (w_up, front.at[1]), (p_gate, probes.at[0]), (p_up, probes.at[1]),
             (w_down, down.at[0]), (p_down, down.at[1]),
+        ])
+    ]
+    states = [
+        pltpu.make_async_copy(src, dst, state_sem.at[i])
+        for i, (src, dst) in enumerate([
+            (m_down, new_moment), (s_down, new_second), (m_gate, moments.at[0]), (s_gate, seconds.at[0]),
+            (m_up, moments.at[1]), (s_up, seconds.at[1]),
         ])
     ]
     for load in loads:
@@ -127,11 +150,14 @@
         @pl.loop(0, hidden // tile_f)
         def _(j):
             cols = pl.ds(pl.multiple_of(j * tile_f, tile_f), tile_f)
-            value = dot(xg[...], front[a, :, cols], (1, 0))
+            weight = front[a, :, cols] if a < 2 else probes[a - 2, :, cols]
+            value = dot(xg[...], weight, (1, 0))
             part[a, :, :, cols] = value.astype(BF16).reshape(n_col, tokens // n_col, tile_f)
 
         col_each(lambda a, k: part_copy(a, k).start(), a)
 
+    for state in states:
+        state.start()
     total = sq_send[c]
     for k in range(1, n_col):
         sq_copy(k).wait_recv()
@@ -208,7 +234,7 @@
     col_each(lambda k: sc_copy(k).wait_recv())
     scales = scale_all[...].reshape(tokens, 128)[:, :1]
     feats = x_all[...].reshape(tokens, width).astype(F32)
-    normed_ref[...] = (feats * scales * gain_ref[...]).astype(BF16)
+    normed_ref[...] = (feats * scales * gain_ref[...]).astype(BF16).T
 
     def back_product(a, make):
         @pl.loop(0, hidden // tile_f)
@@ -226,6 +252,23 @@
         lambda rows: dot(flat(err_ref, 1), down[0, rows, :], (1, 1))
         + dot(flat(err_ref, 0), down[1, rows, :], (1, 1)),
     )
+
+    states[0].wait()
+    states[1].wait()
+
+    @pl.loop(0, hidden // TILE)
+    def _(i):
+        rows = pl.ds(pl.multiple_of(i * TILE, TILE), TILE)
+        primal = hid_ref[0, :, :, rows].reshape(tokens, TILE).T
+        tangent = hid_ref[1, :, :, rows].reshape(tokens, TILE).T
+        for j in range(width // tile_d):
+            cols = slice(j * tile_d, (j + 1) * tile_d)
+            error = err_ref[0, :, :, cols].reshape(tokens, tile_d)
+            error_tan = err_ref[1, :, :, cols].reshape(tokens, tile_d)
+            grad = dot(primal, error, (1, 0))
+            curve = dot(tangent, error, (1, 0)) + dot(primal, error_tan, (1, 0))
+            values = update(new_moment[rows, cols], new_second[rows, cols], down[1, rows, cols], grad, curve)
+            new_moment[rows, cols], new_second[rows, cols], step[rows, cols] = values
 
     back_hidden = summed(bk_part, bk_in, bk_copy, 0)
     back_ref[0, c] = (back_hidden * coef[1]).astype(BF16)
@@ -238,6 +281,8 @@
     back_ref[3, c] = (back_tan * coef[0] + back_hidden * coef[4]).astype(BF16)
     col_each(lambda a, k: back_copy(a, k).start(), 3)
 
+    for state in states[2:]:
+        state.wait()
     for a in range(4):
         col_each(lambda a, k: back_copy(a, k).wait_recv(), a)
 
@@ -259,30 +304,21 @@
             bk_copy(a, k).wait_send()
 
 
-def run_exchange(mesh, x, t, gain, w_gate, w_up, w_down, p_gate, p_up, p_down):
+def run_exchange(mesh, x, t, gain, *large):
     n_row, n_col, n_depth = mesh.shape["row"], mesh.shape["col"], mesh.shape["depth"]
     n_group = n_row * n_depth
     rows, width = x.shape
-    hidden = w_gate.shape[1]
+    hidden = large[0].shape[1]
     tokens = rows * n_group
     run = tokens // n_col
     vmem = pl.BlockSpec(memory_space=pltpu.VMEM)
-    hbm = pl.BlockSpec(memory_space=pl.ANY)
+    hbm = pl.BlockSpec(memory_space=pltpu.HBM)
     sem = pltpu.SemaphoreType.DMA
     pair = lambda *shape: [sem(shape), sem(shape)]
-    shape = jax.ShapeDtypeStruct
-    return pl.pallas_call(
-        functools.partial(exchange, n_row, n_col, n_depth),
-        out_shape=(
-            shape((tokens, width), BF16),
-            shape((2, n_col, run, hidden), BF16),
-            shape((2, n_group, rows, width), BF16),
-            shape((4, n_col, run, hidden), BF16),
-        ),
-        in_specs=[vmem] * 3 + [hbm] * 6,
-        out_specs=(vmem,) * 4,
-        scratch_shapes=[
-            pltpu.VMEM((4, width, hidden), BF16),
+    buffers = [
+            pltpu.VMEM((2, n_col, run, hidden), BF16),
+            pltpu.VMEM((2, n_group, rows, width), BF16),
+            pltpu.VMEM((2, width, hidden), BF16),
             pltpu.VMEM((2, hidden, width), BF16),
             pltpu.VMEM((n_group, rows, width), BF16),
             pltpu.VMEM((tokens, width), BF16),
@@ -296,98 +332,124 @@
             pltpu.VMEM((2, n_group, rows, width), BF16),
             pltpu.VMEM((2, n_col, run, hidden), BF16),
             pltpu.VMEM((2, n_col, run, hidden), BF16),
+    ]
+    size = sum(math.prod(b.shape) * jnp.dtype(b.dtype).itemsize for b in buffers)
+    limit = size + 2**20 + 8 * tokens * width
+    held = pl.pallas_call(
+        functools.partial(exchange, n_row, n_col, n_depth),
+        out_shape=(
+            pltpu.VMEM((width, tokens), BF16),
+            pltpu.VMEM((4, n_col, run, hidden), BF16),
+            pltpu.VMEM((2, width, hidden), BF16),
+            pltpu.VMEM((2, width, hidden), F32),
+            pltpu.VMEM((2, width, hidden), F32),
+            *[pltpu.VMEM((hidden, width), F32)] * 3,
+        ),
+        in_specs=[vmem] * 3 + [hbm] * len(large),
+        out_specs=(vmem,) * 8,
+        scratch_shapes=[
+            *buffers,
+            sem((6,)),
             sem((6,)),
             *pair(n_group), *pair(n_col), *pair(n_col), *pair(4, n_col), *pair(2, n_col),
             *pair(2, n_group), *pair(2, n_group), *pair(2, n_col), *pair(4, n_col),
         ],
         compiler_params=pltpu.CompilerParams(
-            collective_id=0, has_side_effects=True, vmem_limit_bytes=56 * 2**20
+            collective_id=0, has_side_effects=True, vmem_limit_bytes=limit
         ),
-    )(x, t, gain.reshape(1, width), w_gate, w_up, w_down, p_gate, p_up, p_down)
-
-
-def update_tile(moment, second, probe, grad, curve, new_moment, new_second, step, cols):
-    product = probe[:, cols].astype(F32) * curve
-    average = jnp.sum(product) * (1.0 / (TILE * TILE))
-    moved = beta_one * moment[:, cols] + (1.0 - beta_one) * grad
-    square = beta_two * second[:, cols] + (1.0 - beta_two) * average * average
-    new_moment[:, cols] = moved
-    new_second[:, cols] = square
-    root = jnp.sqrt(square * (1.0 / (1.0 - beta_two**STEP)))
-    step[:, cols] = moved * (1.0 / (1.0 - beta_one**STEP)) / (root + adam_floor)
-
-
-def update_front(normed, back, moment, second, probe, new_moment, new_second, step):
-    tokens = normed.shape[0]
-    left = normed[...].T
-    breadth = moment.shape[1]
-    for j in range(breadth // TILE):
-        cols = slice(j * TILE, (j + 1) * TILE)
-        grad = dot(left, back[0, 0, :, :, cols].reshape(tokens, TILE), (1, 0))
-        curve = dot(left, back[1, 0, :, :, cols].reshape(tokens, TILE), (1, 0))
-        update_tile(moment, second, probe, grad, curve, new_moment, new_second, step, cols)
-
-
-def update_down(hid, err, moment, second, probe, new_moment, new_second, step):
-    tokens = err.shape[1] * err.shape[2]
-    primal = hid[0].reshape(tokens, TILE).T
-    tangent = hid[1].reshape(tokens, TILE).T
-    breadth = moment.shape[1]
-    for j in range(breadth // TILE):
-        cols = slice(j * TILE, (j + 1) * TILE)
-        error = err[0, :, :, cols].reshape(tokens, TILE)
-        error_tan = err[1, :, :, cols].reshape(tokens, TILE)
-        grad = dot(primal, error, (1, 0))
-        curve = dot(tangent, error, (1, 0)) + dot(primal, error_tan, (1, 0))
-        update_tile(moment, second, probe, grad, curve, new_moment, new_second, step, cols)
-
-
-def run_update(body, acts, act_specs, moment, second, probe):
-    height, breadth = moment.shape
-    block = pl.BlockSpec((TILE, breadth), lambda i: (i, 0))
+    )(x, t, gain.reshape(1, width), *(pltpu.with_memory_space_constraint(a, pltpu.HBM) for a in large))
+    return held, limit
+
+
+def finish(
+    normed, back, probes, moments, seconds, down_moment, down_second, down_step,
+    gate_out, up_out, down_out, gate_second, up_second, down_second_out, gate_step, up_step, down_step_out,
+    stage, stage_sem, down_sem,
+):
+    writes = [
+        pltpu.make_async_copy(src, dst, down_sem.at[i])
+        for i, (src, dst) in enumerate([
+            (down_moment, down_out), (down_second, down_second_out), (down_step, down_step_out)
+        ])
+    ]
+    for write in writes:
+        write.start()
+    width, hidden = gate_out.shape
+    tokens = normed.shape[1]
+    tiles = width // TILE
+    tile_f = min(256, hidden)
+
+    def write_back(which, i, slot):
+        rows = pl.ds(pl.multiple_of(i * TILE, TILE), TILE)
+        outs = (up_out, up_second, up_step) if which else (gate_out, gate_second, gate_step)
+        return [
+            pltpu.make_async_copy(stage.at[slot, n], out.at[rows], stage_sem.at[slot, n])
+            for n, out in enumerate(outs)
+        ]
+
+    for which in range(2):
+
+        @pl.loop(0, tiles)
+        def _(i):
+            rows = pl.ds(pl.multiple_of(i * TILE, TILE), TILE)
+            slot = lax.rem(which * tiles + i, 2)
+
+            def drain():
+                for copy in write_back(which, i, slot):
+                    copy.wait()
+
+            if which:
+                drain()
+            else:
+                pl.when(i >= 2)(drain)
+            left = normed[rows, :]
+            for j in range(hidden // tile_f):
+                cols = slice(j * tile_f, (j + 1) * tile_f)
+                grad = dot(left, back[which, :, :, cols].reshape(tokens, tile_f), (1, 0))
+                curve = dot(left, back[which + 2, :, :, cols].reshape(tokens, tile_f), (1, 0))
+                values = update(
+                    moments[which, rows, cols], seconds[which, rows, cols], probes[which, rows, cols], grad, curve
+                )
+                for n, value in enumerate(values):
+                    stage[slot, n, :, cols] = value
+            for copy in write_back(which, i, slot):
+                copy.start()
+
+    for i in (tiles - 2, tiles - 1):
+        for copy in write_back(1, i, (tiles + i) % 2):
+            copy.wait()
+    for write in writes:
+        write.wait()
+
+
+def run_finish(held, front, down, limit):
+    hidden = front[1]
+    vmem = pl.BlockSpec(memory_space=pltpu.VMEM)
+    hbm = pl.BlockSpec(memory_space=pltpu.HBM)
+    shapes = [jax.ShapeDtypeStruct(size, F32) for size in (front, front, down)]
     return pl.pallas_call(
-        body,
-        grid=(height // TILE,),
-        out_shape=(jax.ShapeDtypeStruct(moment.shape, F32),) * 3,
-        in_specs=[*act_specs, block, block, block],
-        out_specs=(block,) * 3,
-        compiler_params=pltpu.CompilerParams(
-            dimension_semantics=("arbitrary",), vmem_limit_bytes=40 * 2**20
-        ),
-    )(*acts, moment, second, probe)
+        finish,
+        out_shape=tuple(shapes) * 3,
+        in_specs=[vmem] * len(held),
+        out_specs=(hbm,) * 9,
+        scratch_shapes=[
+            pltpu.VMEM((2, 3, TILE, hidden), F32),
+            pltpu.SemaphoreType.DMA((2, 3)),
+            pltpu.SemaphoreType.DMA((3,)),
+        ],
+        compiler_params=pltpu.CompilerParams(vmem_limit_bytes=limit),
+    )(*(pltpu.with_memory_space_constraint(a, pltpu.VMEM) for a in held))
 
 
 def shards(
     mesh, inputs, targets, norm_gain, w_gate, w_up, w_down, probe_gate, probe_up, probe_down,
     moment_gate, moment_up, moment_down, second_gate, second_up, second_down,
 ):
-    normed, hid, err, back = run_exchange(
-        mesh, inputs, targets, norm_gain, w_gate, w_up, w_down, probe_gate, probe_up, probe_down
+    held, limit = run_exchange(
+        mesh, inputs, targets, norm_gain, w_gate, w_up, w_down, probe_gate, probe_up, probe_down,
+        moment_gate, moment_up, moment_down, second_gate, second_up, second_down,
     )
-    tokens = normed.shape[0]
-    _, n_col, run, hidden = back.shape
-    pairs = back.reshape(2, 2, n_col, run, hidden)
-    normed_spec = pl.BlockSpec((tokens, TILE), lambda i: (0, i))
-
-    def back_spec(which):
-        return pl.BlockSpec((2, 1, n_col, run, hidden), lambda i: (0, which, 0, 0, 0))
-
-    gate = run_update(
-        update_front, (normed, pairs), (normed_spec, back_spec(0)), moment_gate, second_gate, probe_gate
-    )
-    up = run_update(
-        update_front, (normed, pairs), (normed_spec, back_spec(1)), moment_up, second_up, probe_up
-    )
-    down = run_update(
-        update_down,
-        (hid, err),
-        (
-            pl.BlockSpec((2, n_col, run, TILE), lambda i: (0, 0, 0, i)),
-            pl.BlockSpec(err.shape, lambda i: (0, 0, 0, 0)),
-        ),
-        moment_down, second_down, probe_down,
-    )
-    return (gate[0], up[0], down[0], gate[1], up[1], down[1], gate[2], up[2], down[2])
+    return run_finish(held, moment_gate.shape, moment_down.shape, limit)
 
 
 def solution(mesh):

time: 141 us -> 121 us (0.86)
  local copies, waits for them, and re-layouts: 13.4 us -> 1.29 us
  Pallas kernels: 127 us -> 119 us
    unnamed x26 -> x0, local copies, waits for them, and re-layouts: 12.2 us -> none
    pallas_call x3 -> x1, Pallas kernels: 27.5 us -> 21.3 us  [run_finish(): pl.pallas_call(finish, out_shape=tuple(shapes) * 3, in_specs=[vmem] * len...]
    pallas_call x1, Pallas kernels: 99.2 us -> 97.5 us  [run_exchange(): pl.pallas_call(functools.partial(exchange, n_row, n_col, n_depth), out_sh...]
where the time goes in v2:
time: 121 us
  Pallas kernels  119 us (98%)
  local copies, waits for them, and re-layouts  1.29 us (1%)
    pallas_call x1, Pallas kernels, run_exchange(): pl.pallas_call(functools.partial(exchange, n_row, n_col, n_depth), out_sh...  97.5 us
    pallas_call x1, Pallas kernels, run_finish(): pl.pallas_call(finish, out_shape=tuple(shapes) * 3, in_specs=[vmem] * len...  21.3 us

profile of v2, /device:TPU:29, one launch (start us, length us, event | category | flops | bytes accessed | tf_op | source)
XLA Modules:
  0.0 120.7 jit_solution(16479222326988999848)
XLA Ops:
  0.6 1.3 %reshape.21.gain_ref = f32[1,1280]{1,0:T(1,128)} reshape(f32[1280]{0:T(1024)} %param.17) | data formatting | bytes 10240 | tf_op jit(solution)/shard_map/reshape | solution.py:360
  1.9 97.5 %shard_map.214 = (bf16[1280,128]{1,0:T(8,128)(2,1)S(1)}, bf16[4,4,32,1024]{3,2,1,0:T(8,128)(2,1)S(1)}, bf16[2,1280,1024]{2,1,0:T(8,128)(2,1)S(1)}, f32[2,1280,10...) custom-call(bf16[16,1280]{1,0:T(8,128)(2,1)} %x_ref.1, ...), custom_call_target="tpu_custom_call" | custom-call | tf_op jit(solution)/shard_map/pallas_call | solution.py:338
  99.5 21.3 %shard_map.215 = (f32[1280,1024]{1,0:T(8,128)}, f32[1280,1024]{1,0:T(8,128)}, f32[1024,1280]{1,0:T(8,128)}, f32[1280,1024]{1,0:T(8,128)}, f32[1280,1024]{1,0:T(8...) custom-call(bf16[1280,128]{1,0:T(8,128)(2,1)S(1)} %get-tuple-element.17.normed, ...), custom_call_target="tpu_custom_call" | custom-call | tf_op jit(solution)/shard_map/pallas_call | solution.py:430
